TPU v7x, 256 devices: a whole 4x4x8 slice. The times are simulated.
256 devices in a mesh: row: 32 (over y, z), col: 8 (over x, core).
Axes of the slice: x: 4, y: 4, z: 8, core: 2. Of those that a mesh axis runs over, the one named last changes fastest.
Arguments:
- acts: bfloat16 [6144, 28672], P('col', 'row'), may hold values from -12 to 12
- out_grad: bfloat16 [6144, 8192], P('row', 'col'), may hold values from -12 to 12
- lengths: int32 [8], replicated, may hold values from 1 to 768, 4800 in all
Outputs:
- weight_grad: bfloat16 [28672, 8192], P('row', 'col')
- norms: float32 [8], replicated
All inputs are finite; a program needn't handle non-finite values.
Results may differ from a plain program's by a relative error of at most 0.0013.
Values may be sent and summed in bfloat16 or wider, within the bound.
No kernel may reach another device: no remote copies, remote signals or barrier semaphores. Data moves between devices by JAX's collectives and lax.ppermute only.
A program may use at most 128 MiB of HBM per device.

v0:
```python
import jax
import jax.numpy as jnp
from jax import lax
from jax.sharding import PartitionSpec as P

FF = 28672
D = 8192


def body(acts, out_grad, lengths):
    n_row = lax.axis_size("row")
    n_col = lax.axis_size("col")
    row_idx = lax.axis_index("row")
    col_idx = lax.axis_index("col")
    own_rows = out_grad.shape[0]
    tokens = own_rows * n_row
    seqs = lengths.shape[0]
    seq_len = tokens // seqs
    block = own_rows // n_col
    feats = acts.shape[1]
    width = out_grad.shape[1]
    positions = jnp.arange(tokens, dtype=jnp.int32)
    seq_of = positions // seq_len
    limit = jnp.sum(
        jnp.where(
            seq_of[:, None] == jnp.arange(seqs, dtype=jnp.int32)[None, :], lengths[None, :], 0
        ),
        axis=1,
    )
    live = positions % seq_len < limit
    act_full = lax.all_gather(acts, "col", axis=0, tiled=True)
    grad_full = lax.all_gather(out_grad, "row", axis=0, tiled=True)
    grads = jnp.where(live[:, None], grad_full, jnp.zeros_like(grad_full))
    act_seq = act_full.reshape(seqs, seq_len, feats)
    picked = lax.dynamic_index_in_dim(
        act_full.reshape(n_row, n_col, block, feats), col_idx, 1, keepdims=False
    )
    picked = picked.reshape(seqs, n_row // seqs * block, feats)
    act_part = jnp.einsum("sqf,slf->sql", picked, act_seq, preferred_element_type=jnp.float32)
    act_part = act_part.reshape(n_row * block, seq_len)
    summed = lax.psum(act_part.astype(jnp.bfloat16), "row").astype(jnp.float32)
    act_gram = lax.dynamic_slice_in_dim(summed, row_idx * block, block, 0)
    first = row_idx * own_rows
    own_seq = first // seq_len
    own_grads = lax.dynamic_slice_in_dim(grads, first, own_rows, 0)
    seq_grads = lax.dynamic_slice_in_dim(grads, own_seq * seq_len, seq_len, 0)
    grad_part = lax.dot_general(
        own_grads, seq_grads, (((1,), (1,)), ((), ())), preferred_element_type=jnp.float32
    )
    grad_gram = lax.psum_scatter(
        grad_part.astype(jnp.bfloat16), "col", scatter_dimension=0, tiled=True
    ).astype(jnp.float32)
    local = jnp.sum(act_gram * grad_gram)
    onehot = jnp.arange(seqs, dtype=jnp.int32) == own_seq
    squares = lax.psum(jnp.where(onehot, local, jnp.float32(0.0)), ("row", "col"))
    divisor = float(FF) * float(D) * float(seq_len)
    norms = jnp.sqrt(squares / divisor)
    scale = 1.0 / (norms + 0.1)
    total = jnp.zeros((feats, width), jnp.float32)
    for seq in range(seqs):
        act_rows = act_full[seq * seq_len : (seq + 1) * seq_len]
        grad_rows = grads[seq * seq_len : (seq + 1) * seq_len]
        product = lax.dot_general(
            act_rows, grad_rows, (((0,), (0,)), ((), ())), preferred_element_type=jnp.float32
        )
        total = total + scale[seq] * product
    weight_grad = (total / jnp.sqrt(jnp.float32(tokens))).astype(jnp.bfloat16)
    return (weight_grad, norms)


def solution(mesh):
    placed = (P("col", "row"), P("row", "col"), P())
    return jax.shard_map(
        body, mesh=mesh, in_specs=placed, out_specs=(P("row", "col"), P()), check_vma=False
    )
```

profile of v0, /device:TPU:1, one launch (start us, length us, event | category | flops | bytes accessed | tf_op | source)
XLA Modules:
  0.0 495.1 jit_solution(12963730170209471229)
XLA Ops:
  7.2 0.0 all-gather.3.cloned.1.call-start
  7.2 0.7 all-gather.3.cloned.1.call-update
  7.9 0.0 all-gather.5.cloned.1.call-start
  7.9 0.7 all-gather.5.cloned.1.call-update
  8.6 0.0 all-reduce.2.cloned.1.call-start
  8.7 0.8 select_reduce_fusion
  9.6 67.7 %all-gather.3.cloned.1.call-done = bf16[6144,896]{1,0:T(8,128)(2,1)} async-done(((bf16[768,896]{1,0:T(8,128)(2,1)}), bf16[6144,896]{1,0:T(8,128)(2,1)}) %all-gather.3.cloned.1.call-update) | async-done | bytes 11010064 | tf_op jit(solution)/shard_map/all_gather | solution.py:31
  77.2 1.5 constant_dynamic-slice_fusion
  78.7 8.6 %convolution_convert_fusion = bf16[8,96,768]{2,1,0:T(8,128)(2,1)} fusion(bf16[8,96,896]{2,1,0:T(8,128)(2,1)S(1)} %bitcast.20, bf16[8,768,896]{2,1,0:T(8,128)(2,1)} %bitcast.19), kind=kOutput, calls=%fused_computation.20 | convolution fusion | flops 1057554432 | bytes 13565952 | tf_op jit(solution)/shard_map/sqf,slf->sql/dot_general | solution.py:39
  87.3 0.0 all-reduce.2.cloned.1.call-update
  87.4 0.2 reduce-scatter.2.cloned.1.call-start
  87.6 110.4 %all-gather.5.cloned.1.call-done = bf16[6144,1024]{1,0:T(8,128)(2,1)} async-done(((bf16[192,1024]{1,0:T(8,128)(2,1)}), bf16[6144,1024]{1,0:T(8,128)(2,1)}) %all-gather.5.cloned.1.call-update) | async-done | bytes 12582928 | tf_op jit(solution)/shard_map/all_gather | solution.py:32
  197.9 6.4 %broadcast_select_fusion = bf16[6144,1024]{1,0:T(8,128)(2,1)S(1)} fusion(bf16[6144,1024]{1,0:T(8,128)(2,1)} %all-gather.5.cloned.1.call-done, pred[6144]{0:T(1024)(128)(4,1)S(1)} %fusion.32), kind=kLoop, calls=%fused_computation | loop fusion | flops 6291456 | bytes 25171968 | tf_op jit(solution)/shard_map/jit(_where)/select_n | solution.py:33
  204.3 4.5 copy-done
  208.9 1.4 fusion.28
  210.3 0.0 reduce-scatter.2.cloned.1.call-update
  210.3 5.7 %fusion.1 = f32[1024,896]{1,0:T(8,128)} fusion(bf16[6144,1024]{1,0:T(8,128)(2,1)} %copy-done, bf16[6144,896]{1,0:T(8,128)(2,1)} %all-gather.3.cloned.1.call-done), kind=kOutput, calls=%fused_computation.3 | convolution fusion | flops 1409286144 | bytes 6619136 | tf_op jit(solution)/shard_map/dot_general | solution.py:63
  216.0 5.7 %fusion.3 = f32[1024,896]{1,0:T(8,128)} fusion(bf16[6144,1024]{1,0:T(8,128)(2,1)} %copy-done, bf16[6144,896]{1,0:T(8,128)(2,1)} %all-gather.3.cloned.1.call-done), kind=kOutput, calls=%fused_computation.5 | convolution fusion | flops 1409286144 | bytes 6619136 | tf_op jit(solution)/shard_map/dot_general | solution.py:63
  221.7 5.0 %fusion.5 = f32[1024,896]{1,0:T(8,128)} fusion(bf16[6144,1024]{1,0:T(8,128)(2,1)S(1)} %copy-done.1, bf16[6144,896]{1,0:T(8,128)(2,1)} %all-gather.3.cloned.1.call-done), kind=kOutput, calls=%fused_computation.7 | convolution fusion | flops 1409286144 | bytes 6619136 | tf_op jit(solution)/shard_map/dot_general | solution.py:63
  226.7 5.1 %fusion.7 = f32[1024,896]{1,0:T(8,128)} fusion(bf16[6144,1024]{1,0:T(8,128)(2,1)S(1)} %copy-done.1, bf16[6144,896]{1,0:T(8,128)(2,1)} %all-gather.3.cloned.1.call-done), kind=kOutput, calls=%fused_computation.9 | convolution fusion | flops 1409286144 | bytes 6619136 | tf_op jit(solution)/shard_map/dot_general | solution.py:63
  231.9 5.0 %fusion.9 = f32[1024,896]{1,0:T(8,128)} fusion(bf16[6144,1024]{1,0:T(8,128)(2,1)S(1)} %copy-done.1, bf16[6144,896]{1,0:T(8,128)(2,1)} %all-gather.3.cloned.1.call-done), kind=kOutput, calls=%fused_computation.11 | convolution fusion | flops 1409286144 | bytes 6619136 | tf_op jit(solution)/shard_map/dot_general | solution.py:63
  236.9 5.0 %fusion.11 = f32[1024,896]{1,0:T(8,128)} fusion(bf16[6144,1024]{1,0:T(8,128)(2,1)S(1)} %copy-done.1, bf16[6144,896]{1,0:T(8,128)(2,1)} %all-gather.3.cloned.1.call-done), kind=kOutput, calls=%fused_computation.13 | convolution fusion | flops 1409286144 | bytes 6619136 | tf_op jit(solution)/shard_map/dot_general | solution.py:63
  241.8 103.9 %all-reduce.2.cloned.1.call-done = bf16[768,768]{1,0:T(8,128)(2,1)} async-done(((bf16[768,768]{1,0:T(8,128)(2,1)}), bf16[768,768]{1,0:T(8,128)(2,1)}) %all-reduce.2.cloned.1.call-update) | async-done | bytes 1179664 | tf_op jit(solution)/shard_map/psum | solution.py:41
  345.7 35.8 %reduce-scatter.2.cloned.1.call-done = bf16[24,768]{1,0:T(8,128)(2,1)} async-done(((bf16[192,768]{1,0:T(8,128)(2,1)}), bf16[24,768]{1,0:T(8,128)(2,1)}) %reduce-scatter.2.cloned.1.call-update) | async-done | bytes 36880 | tf_op jit(solution)/shard_map/reduce_scatter | solution.py:50
  381.5 1.4 multiply_reduce_fusion
  382.9 0.6 compare_select_fusion
  383.5 5.5 %fusion.13 = f32[1024,896]{1,0:T(8,128)} fusion(bf16[6144,1024]{1,0:T(8,128)(2,1)} %copy-done, bf16[6144,896]{1,0:T(8,128)(2,1)} %all-gather.3.cloned.1.call-done), kind=kOutput, calls=%fused_computation.15 | convolution fusion | flops 1409286144 | bytes 6619136 | tf_op jit(solution)/shard_map/dot_general | solution.py:63
  389.0 78.5 %psum.15 = f32[8]{0:T(128)S(1)} all-reduce(f32[8]{0:T(128)S(1)} %compare_select_fusion), channel_id=1, replica_groups=mesh['row'=32,'col'=8] {'row','col'}, use_global_device_ids=true, to_apply=%region_4.5 | all-reduce | flops 8 | bytes 64 | tf_op jit(solution)/shard_map/psum | solution.py:55
  467.5 0.5 add_divide_fusion
  468.0 0.6 fusion.39
  468.6 17.5 %fusion.17 = bf16[896,1024]{0,1:T(8,128)(2,1)S(1)} fusion(bf16[6144,1024]{1,0:T(8,128)(2,1)} %copy-done, f32[]{:T(128)} %bitcast.11, f32[1024,896]{1,0:T(8,128)} %fusion.1, f32[]{:T(128)} %bitcast.10, f32[1024,896]{1,0:T(8,128)} %fusion.3, f32[]{:T(128)} %bitcast.9, f32[1024,896]{1,0:T(8,128)} %fusion.5, f32[]{:T(128)} %bitcast.8, f32[1024,896]{1,0:T(8,128)} %fusion.7, ...), kind=kOutput, calls=%fused_computation.19 | convolution fusion | flops 1424883712 | bytes 30478336 | tf_op jit(solution)/shard_map/dot_general | solution.py:63
  486.1 2.4 copy.8
  (5 shorter events, 0.0 us)
Async XLA Ops:
  7.2 70.1 %all-gather.3.cloned.1.call-start = ((), (), s32[]{:S(2)}) async-start(), calls=%async_computation.1 | async-start | bytes 12386304 | tf_op jit(solution)/shard_map/all_gather | solution.py:31
  7.9 190.0 %all-gather.5.cloned.1.call-start = ((), (), s32[]{:S(2)}) async-start(), calls=%async_computation.3 | async-start | bytes 12976128 | tf_op jit(solution)/shard_map/all_gather | solution.py:32
  8.6 337.1 %all-reduce.2.cloned.1.call-start = ((), (), s32[]{:S(2)}) async-start(), calls=%async_computation.2 | async-start | bytes 2359296 | tf_op jit(solution)/shard_map/psum | solution.py:41
  87.4 294.1 %reduce-scatter.2.cloned.1.call-start = ((), (), s32[]{:S(2)}) async-start(), calls=%async_computation.4 | async-start | bytes 331776 | tf_op jit(solution)/shard_map/reduce_scatter | solution.py:50
  204.3 4.6 copy-start
  210.3 11.4 %copy-start.1 = (bf16[6144,1024]{1,0:T(8,128)(2,1)S(1)}, bf16[6144,1024]{1,0:T(8,128)(2,1)}, u32[]{:S(2)}) copy-start(bf16[6144,1024]{1,0:T(8,128)(2,1)} %copy-done) | copy-start | bytes 37748740
Sparse Core Ops, SparseCore 0:
  9.8 67.3 all-gather.2
  79.8 118.0 all-gather.4
  201.9 143.7 all-reduce.1
  348.1 33.3 reduce-scatter.1
where the time goes:
time: 496 us; the launch traced here: 495 us
  waiting for transfers between devices  319 us (64%)
  blocking collectives  78.5 us (16%)
  matrix products  64.5 us (13%)
  between operations  13.9 us (3%)
  other arithmetic  9.76 us (2%)
  local copies, waits for them, and re-layouts  9.06 us (2%)
    all_gather x1, waiting for transfers between devices, body(): grad_full = lax.all_gather(out_grad, 'row', axis=0, tiled=True)  110 us
    psum x1, waiting for transfers between devices, body(): summed = lax.psum(act_part.astype(jnp.bfloat16), 'row').astype(jnp.float32)  104 us
    psum x1, blocking collectives, body(): lax.psum(jnp.where(onehot, local, jnp.float32(0.0)), ('row', 'col'))  78.5 us
    all_gather x1, waiting for transfers between devices, body(): act_full = lax.all_gather(acts, 'col', axis=0, tiled=True)  67.7 us
    dot_general x8, matrix products, body(): lax.dot_general(act_rows, grad_rows, (((0,), (0,)), ((), ())), preferred_...  54.5 us
    reduce_scatter x1, waiting for transfers between devices, body(): lax.psum_scatter(grad_part.astype(jnp.bfloat16), 'col', scatter_dimension...  35.8 us
  transfers between devices with their start and end apart: 4, of which 4 were waited for; matrix products, arithmetic and copies ran while one was open for 10% of the time, Pallas kernels for 0%

commit v1 on v0

--- a/solution.py
+++ b/solution.py
@@ -52,7 +52,9 @@
     ).astype(jnp.float32)
     local = jnp.sum(act_gram * grad_gram)
     onehot = jnp.arange(seqs, dtype=jnp.int32) == own_seq
-    squares = lax.psum(jnp.where(onehot, local, jnp.float32(0.0)), ("row", "col"))
+    squares = jnp.sum(
+        lax.all_gather(jnp.where(onehot, local, jnp.float32(0.0)), ("row", "col")), axis=0
+    )
     divisor = float(FF) * float(D) * float(seq_len)
     norms = jnp.sqrt(squares / divisor)
     scale = 1.0 / (norms + 0.1)

time: 496 us -> 471 us (0.950)
  blocking collectives: 78.5 us -> 59.2 us
  matrix products: 64.5 us -> 58.9 us
    psum x1 -> x0, blocking collectives: 78.5 us -> none  [body(): lax.psum(jnp.where(onehot, local, jnp.float32(0.0)), ('row', 'col'))]
    all_gather x0 -> x1, blocking collectives: none -> 59.2 us  [body(): lax.all_gather(jnp.where(onehot, local, jnp.float32(0.0)), ('row', 'col'))]
    dot_general x8, matrix products: 54.5 us -> 48.9 us  [body(): lax.dot_general(act_rows, grad_rows, (((0,), (0,)), ((), ())), preferred_...]
  transfers between devices with their start and end apart: 4 -> 4, of which waited for: 4 -> 4; matrix products, arithmetic and copies ran while one was open for 10% -> 11% of each run, Pallas kernels for 0% -> 0%
where the time goes in v1:
time: 471 us
  waiting for transfers between devices  319 us (68%)
  blocking collectives  59.2 us (13%)
  matrix products  58.9 us (13%)
  between operations  13.9 us (3%)
  other arithmetic  10.1 us (2%)
  local copies, waits for them, and re-layouts  9.07 us (2%)
    all_gather x1, waiting for transfers between devices, body(): grad_full = lax.all_gather(out_grad, 'row', axis=0, tiled=True)  110 us
    psum x1, waiting for transfers between devices, body(): summed = lax.psum(act_part.astype(jnp.bfloat16), 'row').astype(jnp.float32)  104 us
    all_gather x1, waiting for transfers between devices, body(): act_full = lax.all_gather(acts, 'col', axis=0, tiled=True)  67.7 us
    all_gather x1, blocking collectives, body(): lax.all_gather(jnp.where(onehot, local, jnp.float32(0.0)), ('row', 'col'))  59.2 us
    dot_general x8, matrix products, body(): lax.dot_general(act_rows, grad_rows, (((0,), (0,)), ((), ())), preferred_...  48.9 us
    reduce_scatter x1, waiting for transfers between devices, body(): lax.psum_scatter(grad_part.astype(jnp.bfloat16), 'col', scatter_dimension...  35.8 us
  transfers between devices with their start and end apart: 4, of which 4 were waited for; matrix products, arithmetic and copies ran while one was open for 11% of the time, Pallas kernels for 0%

profile of v1, /device:TPU:1, one launch (start us, length us, event | category | flops | bytes accessed | tf_op | source)
XLA Modules:
  0.0 470.8 jit_solution(16397741176272907447)
XLA Ops:
  7.2 0.0 all-gather.4.cloned.1.call-start
  7.2 0.7 all-gather.4.cloned.1.call-update
  7.9 0.0 all-gather.6.cloned.1.call-start
  7.9 0.7 all-gather.6.cloned.1.call-update
  8.6 0.0 all-reduce.2.cloned.1.call-start
  8.7 0.8 select_reduce_fusion
  9.6 67.7 %all-gather.4.cloned.1.call-done = bf16[6144,896]{1,0:T(8,128)(2,1)} async-done(((bf16[768,896]{1,0:T(8,128)(2,1)}), bf16[6144,896]{1,0:T(8,128)(2,1)}) %all-gather.4.cloned.1.call-update) | async-done | bytes 11010064 | tf_op jit(solution)/shard_map/all_gather | solution.py:31
  77.2 1.5 constant_dynamic-slice_fusion
  78.7 8.6 %convolution_convert_fusion = bf16[8,96,768]{2,1,0:T(8,128)(2,1)} fusion(bf16[8,96,896]{2,1,0:T(8,128)(2,1)S(1)} %bitcast.24, bf16[8,768,896]{2,1,0:T(8,128)(2,1)} %bitcast.21), kind=kOutput, calls=%fused_computation.20 | convolution fusion | flops 1057554432 | bytes 13565952 | tf_op jit(solution)/shard_map/sqf,slf->sql/dot_general | solution.py:39
  87.3 0.0 all-reduce.2.cloned.1.call-update
  87.4 0.2 reduce-scatter.2.cloned.1.call-start
  87.6 110.4 %all-gather.6.cloned.1.call-done = bf16[6144,1024]{1,0:T(8,128)(2,1)} async-done(((bf16[192,1024]{1,0:T(8,128)(2,1)}), bf16[6144,1024]{1,0:T(8,128)(2,1)}) %all-gather.6.cloned.1.call-update) | async-done | bytes 12582928 | tf_op jit(solution)/shard_map/all_gather | solution.py:32
  197.9 6.4 %broadcast_select_fusion = bf16[6144,1024]{1,0:T(8,128)(2,1)S(1)} fusion(bf16[6144,1024]{1,0:T(8,128)(2,1)} %all-gather.6.cloned.1.call-done, pred[6144]{0:T(1024)(128)(4,1)S(1)} %fusion.32), kind=kLoop, calls=%fused_computation | loop fusion | flops 6291456 | bytes 25171968 | tf_op jit(solution)/shard_map/jit(_where)/select_n | solution.py:33
  204.3 4.5 copy-done
  208.8 1.4 fusion.28
  210.3 5.7 %fusion.1 = f32[1024,896]{1,0:T(8,128)} fusion(bf16[6144,1024]{1,0:T(8,128)(2,1)} %copy-done, bf16[6144,896]{1,0:T(8,128)(2,1)} %all-gather.4.cloned.1.call-done), kind=kOutput, calls=%fused_computation.3 | convolution fusion | flops 1409286144 | bytes 6619136 | tf_op jit(solution)/shard_map/dot_general | solution.py:65
  216.0 5.7 %fusion.3 = f32[1024,896]{1,0:T(8,128)} fusion(bf16[6144,1024]{1,0:T(8,128)(2,1)} %copy-done, bf16[6144,896]{1,0:T(8,128)(2,1)} %all-gather.4.cloned.1.call-done), kind=kOutput, calls=%fused_computation.5 | convolution fusion | flops 1409286144 | bytes 6619136 | tf_op jit(solution)/shard_map/dot_general | solution.py:65
  221.7 5.1 %fusion.5 = f32[1024,896]{1,0:T(8,128)} fusion(bf16[6144,1024]{1,0:T(8,128)(2,1)S(1)} %copy-done.1, bf16[6144,896]{1,0:T(8,128)(2,1)} %all-gather.4.cloned.1.call-done), kind=kOutput, calls=%fused_computation.7 | convolution fusion | flops 1409286144 | bytes 6619136 | tf_op jit(solution)/shard_map/dot_general | solution.py:65
  226.9 3.7 fusion.7
  230.6 3.7 fusion.9
  234.3 3.6 fusion.11
  237.9 3.7 fusion.13
  241.6 104.1 %all-reduce.2.cloned.1.call-done = bf16[768,768]{1,0:T(8,128)(2,1)} async-done(((bf16[768,768]{1,0:T(8,128)(2,1)}), bf16[768,768]{1,0:T(8,128)(2,1)}) %all-reduce.2.cloned.1.call-update) | async-done | bytes 1179664 | tf_op jit(solution)/shard_map/psum | solution.py:41
  345.7 35.8 %reduce-scatter.2.cloned.1.call-done = bf16[24,768]{1,0:T(8,128)(2,1)} async-done(((bf16[192,768]{1,0:T(8,128)(2,1)}), bf16[24,768]{1,0:T(8,128)(2,1)}) %reduce-scatter.2.cloned.1.call-update) | async-done | bytes 36880 | tf_op jit(solution)/shard_map/reduce_scatter | solution.py:50
  381.5 1.4 multiply_reduce_fusion
  382.9 0.6 fusion.39
  383.5 59.2 %all-gather = f32[256,1,8]{2,1,0:T(1,128)S(1)} all-gather(f32[1,1,8]{2,1,0:T(1,128)S(1)} %fusion.39), channel_id=1, replica_groups=mesh['row'=32,'col'=8] {'row','col'}, dimensions={0}, use_global_device_ids=true | all-gather | bytes 8224 | tf_op jit(solution)/shard_map/all_gather | solution.py:56
  442.8 0.3 reduce_sum.29
  443.0 0.5 add_divide_fusion
  443.6 0.7 fusion.40
  444.2 17.6 %fusion.17 = bf16[896,1024]{0,1:T(8,128)(2,1)S(1)} fusion(bf16[6144,1024]{1,0:T(8,128)(2,1)} %copy-done, f32[]{:T(128)} %bitcast.12, f32[1024,896]{1,0:T(8,128)} %fusion.1, f32[]{:T(128)} %bitcast.11, f32[1024,896]{1,0:T(8,128)} %fusion.3, f32[]{:T(128)} %bitcast.10, f32[1024,896]{1,0:T(8,128)} %fusion.5, f32[]{:T(128)} %bitcast.9, f32[1024,896]{1,0:T(8,128)} %fusion.7, ...), kind=kOutput, calls=%fused_computation.19 | convolution fusion | flops 1424883712 | bytes 30478336 | tf_op jit(solution)/shard_map/dot_general | solution.py:65
  461.9 2.4 copy.10
  (13 shorter events, 0.1 us)
Async XLA Ops:
  7.2 70.1 %all-gather.4.cloned.1.call-start = ((), (), s32[]{:S(2)}) async-start(), calls=%async_computation.1 | async-start | bytes 12386304 | tf_op jit(solution)/shard_map/all_gather | solution.py:31
  7.9 190.0 %all-gather.6.cloned.1.call-start = ((), (), s32[]{:S(2)}) async-start(), calls=%async_computation.3 | async-start | bytes 12976128 | tf_op jit(solution)/shard_map/all_gather | solution.py:32
  8.6 337.1 %all-reduce.2.cloned.1.call-start = ((), (), s32[]{:S(2)}) async-start(), calls=%async_computation.2 | async-start | bytes 2359296 | tf_op jit(solution)/shard_map/psum | solution.py:41
  87.4 294.1 %reduce-scatter.2.cloned.1.call-start = ((), (), s32[]{:S(2)}) async-start(), calls=%async_computation.4 | async-start | bytes 331776 | tf_op jit(solution)/shard_map/reduce_scatter | solution.py:50
  204.3 4.5 copy-start
  210.3 11.4 %copy-start.1 = (bf16[6144,1024]{1,0:T(8,128)(2,1)S(1)}, bf16[6144,1024]{1,0:T(8,128)(2,1)}, u32[]{:S(2)}) copy-start(bf16[6144,1024]{1,0:T(8,128)(2,1)} %copy-done) | copy-start | bytes 37748740
  216.0 10.9 %slice-start = ((s8[11010048]{0:T(1024)(128)(4,1)}), s8[4194304]{0:T(1024)(128)(4,1)S(1)}, s32[]{:S(2)}) async-start(s8[11010048]{0:T(1024)(128)(4,1)} %bitcast.22), calls=%async_computation.5 | async-start | bytes 8388608
  216.0 10.9 %slice-start.1 = ((s8[11010048]{0:T(1024)(128)(4,1)}), s8[4194304]{0:T(1024)(128)(4,1)S(1)}, s32[]{:S(2)}) async-start(s8[11010048]{0:T(1024)(128)(4,1)} %bitcast.22), calls=%async_computation.6 | async-start | bytes 8388608
  221.7 5.2 %slice-start.2 = ((s8[11010048]{0:T(1024)(128)(4,1)}), s8[2621440]{0:T(1024)(128)(4,1)S(1)}, s32[]{:S(2)}) async-start(s8[11010048]{0:T(1024)(128)(4,1)} %bitcast.22), calls=%async_computation.7 | async-start | bytes 5242880
Sparse Core Ops, SparseCore 0:
  9.8 67.3 all-gather.3
  79.8 118.0 all-gather.5
  201.9 143.7 all-reduce.1
  348.1 33.3 reduce-scatter.1
